TPU v7x, 256 devices: a whole 4x4x8 slice. The times are simulated.
256 devices in a mesh: dp: 4 (over z_lo), ctx: 64 (over z_hi, x, y, core).
Axes of the slice: x: 4, y: 4, z: 8 (z_hi: 2, z_lo: 4; z = z_hi * 4 + z_lo), core: 2. Of those that a mesh axis runs over, the one named last changes fastest.
Arguments:
- inputs: bfloat16 [4, 16384, 4096], P('dp', 'ctx'), may hold values from -16 to 16
- value_weight: bfloat16 [4096, 512], P('ctx'), may hold values from -0.09375 to 0.09375
- query_states: bfloat16 [4, 16384, 2048], P('dp', 'ctx'), may hold values from -40 to 40
- key_states: bfloat16 [4, 16384, 512], P('dp', 'ctx'), may hold values from -6 to 6
- value_states: bfloat16 [4, 16384, 512], P('dp', 'ctx'), may hold values from -6 to 6
- attention_out: bfloat16 [4, 16384, 2048], P('dp', 'ctx'), may hold values from -4 to 4
- out_grad: bfloat16 [4, 16384, 2048], P('dp', 'ctx'), may hold values from -6 to 6
- segment_ids: int32 [4, 16384], P('dp', 'ctx'), may hold values from 0 to 31, never falling along the last dimension, each value on 1 to 4096 neighbouring positions
Outputs:
- query_grad: bfloat16 [4, 16384, 2048], P('dp', 'ctx')
- key_grad: bfloat16 [4, 16384, 512], P('dp', 'ctx')
- input_grad: bfloat16 [4, 16384, 4096], P('dp', 'ctx')
- weight_grad: float32 [4096, 512], P('ctx')
Inputs may be any that keep to these rules, and one draw needn't show every extreme that they name: `segment_ids`: along each sequence the ids never fall; each record holds 1 to 4096 tokens and one holds exactly 4096.
All inputs are finite; a program needn't handle non-finite values.
Results may differ from a plain program's by a relative error of at most 0.0057.
Values may be sent and summed in bfloat16 or wider, within the bound.
A program may use at most 128 MiB of HBM per device.

v0:
```python
import math
import jax
import jax.numpy as jnp
from jax import lax
from jax.sharding import PartitionSpec as P

HQ = 16
KVH = 4
DH = 128
W = 2048


def carried_in(value, axis, combine, identity):
    peers, here = (lax.axis_size(axis), lax.axis_index(axis))
    everything = jax.tree.map(lambda part: lax.all_gather(part, axis), value)
    start = jax.tree.map(
        lambda part, zero: jnp.broadcast_to(jnp.asarray(zero, part.dtype), part.shape),
        value,
        identity,
    )

    def turn(k, before):
        reached = k < here
        new = combine(before, jax.tree.map(lambda part: part[k], everything))
        return jax.tree.map(lambda a, b: jnp.where(reached, a, b), new, before)

    return lax.fori_loop(0, peers, turn, start)


def passed_along(block, axis, distance):
    devices = range(lax.axis_size(axis))
    route = [(i - distance, i) for i in devices if i - distance in devices]
    return lax.ppermute(block, axis, route)


def link_records(earlier, later):
    first_early, last_early, start_early, whole_early, empty_early = earlier
    first_late, last_late, start_late, whole_late, empty_late = later
    joined = last_early == first_late
    start_merged = jnp.where((whole_late == 1) & joined, start_early, start_late)
    whole_merged = jnp.where((whole_early == 1) & (whole_late == 1) & joined, 1, 0).astype(
        jnp.int32
    )
    merged = (first_early, last_late, start_merged, whole_merged, jnp.zeros_like(empty_early))
    return tuple(
        (
            jnp.where(
                empty_early == 1, late_item, jnp.where(empty_late == 1, early_item, merged_item)
            )
            for early_item, late_item, merged_item in zip(earlier, later, merged)
        )
    )


def attend_group(operands, live_mask, factor):
    query_group, key_group, value_group, grad_group, output_group = operands
    scores = (
        jnp.einsum("gqd,kd->gqk", query_group, key_group, preferred_element_type=jnp.float32)
        * factor
    )
    scores = jnp.where(live_mask[None], scores, -1e30)
    row_max = jnp.max(scores, axis=-1, keepdims=True)
    exp_score = jnp.exp(scores - row_max)
    prob_full = exp_score / jnp.sum(exp_score, axis=-1, keepdims=True)
    prob_low = prob_full.astype(jnp.bfloat16)
    row_delta = jnp.sum(
        grad_group.astype(jnp.float32) * output_group.astype(jnp.float32), axis=-1, keepdims=True
    )
    prob_grad = jnp.einsum(
        "gqd,kd->gqk", grad_group, value_group, preferred_element_type=jnp.float32
    )
    score_grad = (prob_full * (prob_grad - row_delta)).astype(jnp.bfloat16)
    query_part = (
        jnp.einsum("gqk,kd->gqd", score_grad, key_group, preferred_element_type=jnp.float32)
        * factor
    )
    key_part = (
        jnp.einsum("gqk,gqd->kd", score_grad, query_group, preferred_element_type=jnp.float32)
        * factor
    )
    value_part = jnp.einsum("gqk,gqd->kd", prob_low, grad_group, preferred_element_type=jnp.float32)
    return (query_part, key_part, value_part)


def attend_tail(factor, operands):
    query_heads, key_heads, value_heads, grad_heads, output_heads, live_mask = operands
    query_part, key_part, value_part = lax.map(
        lambda head_parts: attend_group(head_parts, live_mask, factor),
        (query_heads, key_heads, value_heads, grad_heads, output_heads),
    )
    return (query_part, key_part, value_part)


def on_device(
    inputs,
    value_weight,
    query_states,
    key_states,
    value_states,
    attention_out,
    out_grad,
    segment_ids,
):
    tok_rows = query_states.shape[1]
    span_blocks = W // tok_rows
    group_size = HQ // KVH
    width_kv = KVH * DH
    factor = 1.0 / math.sqrt(DH)
    window_rows = (span_blocks + 1) * tok_rows
    input_rows = inputs[0]
    values = value_states[0]
    seg_local = segment_ids[0]
    device_index = lax.axis_index("ctx")
    offset = device_index * tok_rows
    before = jnp.sum((seg_local[None, :] < seg_local[:, None]).astype(jnp.int32), axis=1)
    first_id = seg_local[0]
    last_id = seg_local[-1]
    summary = (
        first_id,
        last_id,
        offset + before[-1],
        (first_id == last_id).astype(jnp.int32),
        jnp.zeros((), jnp.int32),
    )
    identity = tuple((jnp.full((), filler, jnp.int32) for filler in (0, 0, 0, 1, 1)))
    prior = carried_in(summary, "ctx", link_records, identity)
    carried = (before == 0) & (prior[4] == 0) & (prior[1] == first_id)
    starts = jnp.where(carried, prior[2], offset + before)
    kv_block = jnp.stack([key_states[0], values])
    blank_window = jnp.zeros((2, window_rows, width_kv), jnp.bfloat16)
    blank_window = lax.dynamic_update_slice_in_dim(
        blank_window, kv_block, span_blocks * tok_rows, 1
    )

    def pass_on(hop_number, carry):
        moving, filled = carry
        moving = passed_along(moving, "ctx", 1)
        filled = lax.dynamic_update_slice_in_dim(
            filled, moving, (span_blocks - hop_number) * tok_rows, 1
        )
        return (moving, filled)

    window = lax.fori_loop(1, span_blocks + 1, pass_on, (kv_block, blank_window))[1]
    key_base = offset - span_blocks * tok_rows
    key_pos = key_base + jnp.arange(window_rows, dtype=jnp.int32)
    query_pos = offset + jnp.arange(tok_rows, dtype=jnp.int32)
    live_mask = (
        (key_pos[None, :] >= starts[:, None])
        & (key_pos[None, :] <= query_pos[:, None])
        & (key_pos[None, :] > query_pos[:, None] - W)
    )
    query_heads = query_states[0].reshape(tok_rows, KVH, group_size, DH).transpose(1, 2, 0, 3)
    grad_heads = out_grad[0].reshape(tok_rows, KVH, group_size, DH).transpose(1, 2, 0, 3)
    output_heads = attention_out[0].reshape(tok_rows, KVH, group_size, DH).transpose(1, 2, 0, 3)
    key_heads = window[0].reshape(window_rows, KVH, DH).transpose(1, 0, 2)
    value_heads = window[1].reshape(window_rows, KVH, DH).transpose(1, 0, 2)
    operands = (query_heads, key_heads, value_heads, grad_heads, output_heads, live_mask)
    query_part, key_part, value_part = attend_tail(factor, operands)
    query_grad = query_part.transpose(2, 0, 1, 3).reshape(1, tok_rows, HQ * DH).astype(jnp.bfloat16)
    grads = jnp.stack(
        [
            key_part.transpose(1, 0, 2).reshape(window_rows, width_kv),
            value_part.transpose(1, 0, 2).reshape(window_rows, width_kv),
        ]
    )

    def return_step(hop_number, carried_sum):
        moved = passed_along(carried_sum, "ctx", -1)
        return moved + lax.dynamic_slice_in_dim(grads, hop_number * tok_rows, tok_rows, 1)

    totals = lax.fori_loop(1, span_blocks + 1, return_step, grads[:, :tok_rows])
    key_grad = totals[0].astype(jnp.bfloat16)[None]
    value_delta = totals[1].astype(jnp.bfloat16)
    input_grad = jnp.einsum(
        "tk,rk->tr",
        value_delta,
        lax.all_gather(value_weight, "ctx", axis=0, tiled=True),
        preferred_element_type=jnp.float32,
    )
    input_grad = input_grad.astype(jnp.bfloat16)[None]
    weight_share = lax.psum_scatter(
        jnp.einsum("tr,tk->rk", input_rows, value_delta, preferred_element_type=jnp.float32),
        "ctx",
        scatter_dimension=0,
        tiled=True,
    )
    weight_grad = lax.psum(weight_share, "dp")
    return (query_grad, key_grad, input_grad, weight_grad)


def solution(mesh):
    placed = (
        P("dp", "ctx", None),
        P("ctx", None),
        P("dp", "ctx", None),
        P("dp", "ctx", None),
        P("dp", "ctx", None),
        P("dp", "ctx", None),
        P("dp", "ctx", None),
        P("dp", "ctx"),
    )
    return jax.shard_map(
        on_device,
        mesh=mesh,
        in_specs=placed,
        out_specs=(
            P("dp", "ctx", None),
            P("dp", "ctx", None),
            P("dp", "ctx", None),
            P("ctx", None),
        ),
        check_vma=False,
    )
```

profile of v0, /device:TPU:2, one launch (start us, length us, event | category | flops | bytes accessed | tf_op | source)
XLA Modules:
  0.0 1700.2 jit_solution(13102222631023237591)
XLA Ops:
  18.7 24.4 %all-reduce.6 = (s32[64]{0:T(128)S(1)}, s32[64]{0:T(128)S(1)}, s32[64]{0:T(128)S(1)}, s32[64]{0:T(128)S(1)}, s32[64]{0:T(128)S(1)}) all-reduce(s32[64]{0:T(128)S(1)} %bitcast_dynamic-update-slice_fusion.1, s32[64]{0:T(128)S(1)} %dynamic-update-slice.1, s32[64]{0:T(128)S(1)} %dynamic-update-slice.2, ...), channel_id=2, replica_groups=mesh['dp'=4,'ctx'=64] {'ctx'}, use_global_device_ids=true, to_apply=%add.1 | all-reduce | flops 320 | bytes 2560 | tf_op jit(solution)/shard_map/all_gather | solution.py:15
  43.1 521.7 %while.60 = (s32[]{:T(128)}, s32[]{:T(128)}, s32[]{:T(128)}, s32[]{:T(128)}, s32[]{:T(128)}, /*index=5*/s32[64]{0:T(128)S(1)}, s32[64]{0:T(128)S(1)}, s32[64]{0:...) while((s32[]{:T(128)}, s32[]{:T(128)}, s32[]{:T(128)}, ...), condition=%wide.region_4.5_spmd, body=%wide.region_3.4_spmd.sunk | while | flops 18 | bytes 363 | solution.py:27
  569.8 107.9 %while.61 = (s32[]{:T(128)}, bf16[2,256,512]{2,1,0:T(8,128)(2,1)S(1)}, bf16[2,2304,512]{2,1,0:T(8,128)(2,1)}, s32[]{:T(128)}, s32[]{:T(128)}, /*index=5*/s32[]{:T(128)}, s32[]{:T(128)}, s32[]{:T(128)}) while((s32[]{:T(128)}, bf16[2,256,512]{2,1,0:T(8,128)(2,1)S(1)}, bf16[2,2304,512]{2,1,0:T(8,128)(2,1)}, s32[]{:T(128)}, s32[]{:T(128)}, ...), condition=%wide.region_1.2_spmd, body=%wide.region_0.0_spmd.sunk | while | flops 7 | bytes 4194491 | solution.py:143
  571.7 10.7 collective-permute-done
  585.2 10.7 collective-permute-done
  598.7 10.7 collective-permute-done
  612.2 10.7 collective-permute-done
  625.7 10.7 collective-permute-done
  639.2 10.7 collective-permute-done
  652.7 10.7 collective-permute-done
  666.1 10.7 collective-permute-done
  695.2 144.7 %while.63 = (s32[]{:T(128)}, bf16[4,4,256,128]{3,2,1,0:T(8,128)(2,1)}, f32[4,2304,128]{1,2,0:T(8,128)}, f32[4,2304,128]{1,2,0:T(8,128)}, bf16[4,4,256,128]{2,3,1...) while((s32[]{:T(128)}, ...), condition=%wide.region_9.10_spmd.clone, body=%wide.region_5.9_spmd.clone.sunk | while | flops 3658453504 | bytes 69966016 | solution.py:87
  697.8 8.6 fusion.117
  733.9 8.6 fusion.117
  760.8 6.8 fusion.120
  770.1 8.6 fusion.117
  806.2 8.6 fusion.117
  833.1 6.8 fusion.120
  839.9 8.8 pad_maximum_fusion
  850.3 163.5 %while.62 = (s32[]{:T(128)}, f32[2,256,512]{2,1,0:T(8,128)}, f32[2,2304,512]{1,2,0:T(8,128)}, s32[]{:T(128)}, s32[]{:T(128)}, /*index=5*/s32[]{:T(128)}, s32[]{:T(128)}) while((s32[]{:T(128)}, f32[2,256,512]{2,1,0:T(8,128)}, f32[2,2304,512]{1,2,0:T(8,128)}, s32[]{:T(128)}, s32[]{:T(128)}, /*index=5*/s32[]{:T(128)}, s32[]{:T(128)}) %tuple.122), condition=%wide.region_11.12_spmd, body=%wide.region_10.11_spmd.sunk | while | flops 262150 | bytes 11534503 | solution.py:171
  856.0 8.8 collective-permute-done.1
  877.0 8.8 collective-permute-done.1
  897.9 8.8 collective-permute-done.1
  918.8 8.8 collective-permute-done.1
  939.8 8.8 collective-permute-done.1
  960.7 8.8 collective-permute-done.1
  981.6 8.8 collective-permute-done.1
  1002.6 8.8 collective-permute-done.1
  1019.3 9.0 copy.72
  1034.6 484.9 %reduce-scatter.4.cloned.1.call-done = f32[64,512]{1,0:T(8,128)} async-done(((f32[4096,512]{1,0:T(8,128)}), f32[64,512]{1,0:T(8,128)}) %reduce-scatter.4.cloned.1.call-update) | async-done | bytes 131088
  1521.2 123.7 %all-gather.4.cloned.1.call-done = bf16[4096,512]{1,0:T(8,128)(2,1)} async-done(((bf16[64,512]{1,0:T(8,128)(2,1)}), bf16[4096,512]{1,0:T(8,128)(2,1)}) %all-gather.4.cloned.1.call-update) | async-done | bytes 4194320 | tf_op jit(solution)/shard_map/all_gather | solution.py:177
  1649.9 42.0 %all-reduce.9.cloned.1.call-done = f32[64,512]{0,1:T(8,128)} async-done(((f32[64,512]{0,1:T(8,128)}), f32[64,512]{0,1:T(8,128)}) %all-reduce.9.cloned.1.call-update) | async-done | bytes 131088 | tf_op jit(solution)/shard_map/psum | solution.py:187
  (485 shorter events, 460.0 us)
Async XLA Ops:
  7.2 1006.6 %copy-start = (bf16[1,256,4096]{2,1,0:T(8,128)(2,1)S(1)}, bf16[1,256,4096]{2,1,0:T(8,128)(2,1)}, u32[]{:S(2)}) copy-start(bf16[1,256,4096]{2,1,0:T(8,128)(2,1)} %param.16) | copy-start | bytes 6291460
  7.2 1512.3 %reduce-scatter.4.cloned.1.call-start = ((), (), s32[]{:S(2)}) async-start(), calls=%async_computation.3 | async-start | bytes 8519680
  569.8 12.6 collective-permute-start
  583.3 12.6 collective-permute-start
  596.8 12.6 collective-permute-start
  610.3 12.6 collective-permute-start
  623.8 12.6 collective-permute-start
  637.3 12.6 collective-permute-start
  650.7 12.6 collective-permute-start
  664.2 12.6 collective-permute-start
  684.4 4.9 copy-start.5
  697.8 8.6 copy-start.4
  711.9 2.1 copy-start.1
  733.9 8.6 copy-start.4
  747.9 2.1 copy-start.1
  770.1 8.6 copy-start.4
  784.1 2.1 copy-start.1
  806.2 8.6 copy-start.4
  820.2 2.1 copy-start.1
  839.9 8.9 copy-start.2
  839.9 9.0 copy-start.3
  850.3 14.5 collective-permute-start.1
  867.2 18.5 %collective-permute-start.1 = (f32[2,256,512]{2,1,0:T(8,128)}, f32[2,256,512]{2,1,0:T(8,128)}, u32[]{:S(2)}, u32[]{:S(2)}) collective-permute-start(f32[2,256,512]{2,1,0:T(8,128)} %get-tuple-element.833), channel_id=1, source_target_pairs={{1,0},{2,1},{3,2},{4,3},{5,4},{6,5},{7,6},{8,7},{9,8},{10,9},{11,1... | collective-permute-start | bytes 3145736 | tf_op jit(solution)/shard_map/while/body/eval_jaxpr/ppermute | solution.py:33
  888.1 18.5 %collective-permute-start.1 = (f32[2,256,512]{2,1,0:T(8,128)}, f32[2,256,512]{2,1,0:T(8,128)}, u32[]{:S(2)}, u32[]{:S(2)}) collective-permute-start(f32[2,256,512]{2,1,0:T(8,128)} %get-tuple-element.833), channel_id=1, source_target_pairs={{1,0},{2,1},{3,2},{4,3},{5,4},{6,5},{7,6},{8,7},{9,8},{10,9},{11,1... | collective-permute-start | bytes 3145736 | tf_op jit(solution)/shard_map/while/body/eval_jaxpr/ppermute | solution.py:33
  909.1 18.5 %collective-permute-start.1 = (f32[2,256,512]{2,1,0:T(8,128)}, f32[2,256,512]{2,1,0:T(8,128)}, u32[]{:S(2)}, u32[]{:S(2)}) collective-permute-start(f32[2,256,512]{2,1,0:T(8,128)} %get-tuple-element.833), channel_id=1, source_target_pairs={{1,0},{2,1},{3,2},{4,3},{5,4},{6,5},{7,6},{8,7},{9,8},{10,9},{11,1... | collective-permute-start | bytes 3145736 | tf_op jit(solution)/shard_map/while/body/eval_jaxpr/ppermute | solution.py:33
  930.0 18.5 %collective-permute-start.1 = (f32[2,256,512]{2,1,0:T(8,128)}, f32[2,256,512]{2,1,0:T(8,128)}, u32[]{:S(2)}, u32[]{:S(2)}) collective-permute-start(f32[2,256,512]{2,1,0:T(8,128)} %get-tuple-element.833), channel_id=1, source_target_pairs={{1,0},{2,1},{3,2},{4,3},{5,4},{6,5},{7,6},{8,7},{9,8},{10,9},{11,1... | collective-permute-start | bytes 3145736 | tf_op jit(solution)/shard_map/while/body/eval_jaxpr/ppermute | solution.py:33
  950.9 18.5 %collective-permute-start.1 = (f32[2,256,512]{2,1,0:T(8,128)}, f32[2,256,512]{2,1,0:T(8,128)}, u32[]{:S(2)}, u32[]{:S(2)}) collective-permute-start(f32[2,256,512]{2,1,0:T(8,128)} %get-tuple-element.833), channel_id=1, source_target_pairs={{1,0},{2,1},{3,2},{4,3},{5,4},{6,5},{7,6},{8,7},{9,8},{10,9},{11,1... | collective-permute-start | bytes 3145736 | tf_op jit(solution)/shard_map/while/body/eval_jaxpr/ppermute | solution.py:33
  971.9 18.5 %collective-permute-start.1 = (f32[2,256,512]{2,1,0:T(8,128)}, f32[2,256,512]{2,1,0:T(8,128)}, u32[]{:S(2)}, u32[]{:S(2)}) collective-permute-start(f32[2,256,512]{2,1,0:T(8,128)} %get-tuple-element.833), channel_id=1, source_target_pairs={{1,0},{2,1},{3,2},{4,3},{5,4},{6,5},{7,6},{8,7},{9,8},{10,9},{11,1... | collective-permute-start | bytes 3145736 | tf_op jit(solution)/shard_map/while/body/eval_jaxpr/ppermute | solution.py:33
  992.8 18.5 %collective-permute-start.1 = (f32[2,256,512]{2,1,0:T(8,128)}, f32[2,256,512]{2,1,0:T(8,128)}, u32[]{:S(2)}, u32[]{:S(2)}) collective-permute-start(f32[2,256,512]{2,1,0:T(8,128)} %get-tuple-element.833), channel_id=1, source_target_pairs={{1,0},{2,1},{3,2},{4,3},{5,4},{6,5},{7,6},{8,7},{9,8},{10,9},{11,1... | collective-permute-start | bytes 3145736 | tf_op jit(solution)/shard_map/while/body/eval_jaxpr/ppermute | solution.py:33
  1028.4 616.6 %all-gather.4.cloned.1.call-start = ((), (), s32[]{:S(2)}) async-start(), calls=%async_computation.1 | async-start | bytes 4259840 | tf_op jit(solution)/shard_map/all_gather | solution.py:177
  1029.1 662.8 %all-reduce.9.cloned.1.call-start = ((), (), s32[]{:S(2)}) async-start(), calls=%async_computation.2 | async-start | bytes 524288 | tf_op jit(solution)/shard_map/psum | solution.py:187
Sparse Core Ops, SparseCore 0:
  1028.5 490.9 reduce-scatter.3
  1523.1 121.7 all-gather.3
  1647.5 44.3 all-reduce.8
where the time goes:
time: 1710 us; the launch traced here: 1700 us
  waiting for transfers between devices  807 us (47%)
  loops' own time  327 us (19%)
  local copies, waits for them, and re-layouts  308 us (18%)
  matrix products  126 us (7%)
  starting transfers between devices  58.7 us (3%)
  other arithmetic  33.3 us (2%)
  blocking collectives  24.4 us (1%)
    unnamed x4, waiting for transfers between devices  486 us
    another operation x1, loops' own time, carried_in(): return lax.fori_loop(0, peers, turn, start)  327 us
    dynamic_slice x320, local copies, waits for them, and re-layouts, turn(): new = combine(before, jax.tree.map(lambda part: part[k], everything))  195 us
    ppermute x16, waiting for transfers between devices, passed_along(): return lax.ppermute(block, axis, route)  156 us
    all_gather x1, waiting for transfers between devices, on_device(): lax.all_gather(value_weight, 'ctx', axis=0, tiled=True)  124 us
    ppermute x16, starting transfers between devices, passed_along(): return lax.ppermute(block, axis, route)  58.6 us
    psum x1, waiting for transfers between devices, on_device(): weight_grad = lax.psum(weight_share, 'dp')  42 us
    sub x4, matrix products, attend_group(): exp_score = jnp.exp(scores - row_max)  34.2 us
  transfers between devices with their start and end apart: 19, of which 19 were waited for; matrix products, arithmetic and copies ran while one was open for 3% of the time, Pallas kernels for 0%

commit v1 on v0

--- a/solution.py
+++ b/solution.py
@@ -184,7 +184,7 @@
         scatter_dimension=0,
         tiled=True,
     )
-    weight_grad = lax.psum(weight_share, "dp")
+    weight_grad = jnp.sum(lax.all_gather(weight_share, "dp"), axis=0)
     return (query_grad, key_grad, input_grad, weight_grad)
 
 

time: 1710 us -> 1570 us (0.918)
  the two profiles are of different devices: /device:TPU:2 before, /device:TPU:0 now
where the time goes in v1:
time: 1570 us
  waiting for transfers between devices  659 us (42%)
  loops' own time  315 us (20%)
  local copies, waits for them, and re-layouts  303 us (19%)
  matrix products  126 us (8%)
  starting transfers between devices  73.1 us (5%)
  blocking collectives  38.8 us (2%)
  other arithmetic  34.6 us (2%)
  between operations  16.8 us (1%)
    reduce_scatter x1, waiting for transfers between devices, on_device(): lax.psum_scatter(jnp.einsum('tr,tk->rk', input_rows, value_delta, preferr...  560 us
    another operation x1, loops' own time, carried_in(): return lax.fori_loop(0, peers, turn, start)  315 us
    dynamic_slice x320, local copies, waits for them, and re-layouts, turn(): new = combine(before, jax.tree.map(lambda part: part[k], everything))  194 us
    ppermute x16, waiting for transfers between devices, passed_along(): return lax.ppermute(block, axis, route)  98 us
    ppermute x16, starting transfers between devices, passed_along(): return lax.ppermute(block, axis, route)  73 us
    sub x4, matrix products, attend_group(): exp_score = jnp.exp(scores - row_max)  34.2 us
  transfers between devices with their start and end apart: 18, of which 17 were waited for; matrix products, arithmetic and copies ran while one was open for 29% of the time, Pallas kernels for 0%

profile of v1, /device:TPU:0, one launch (start us, length us, event | category | flops | bytes accessed | tf_op | source)
XLA Modules:
  0.0 1565.6 jit_solution(8038970534555572962)
XLA Ops:
  19.0 24.0 %all-reduce.6 = (s32[64]{0:T(128)S(1)}, s32[64]{0:T(128)S(1)}, s32[64]{0:T(128)S(1)}, s32[64]{0:T(128)S(1)}, s32[64]{0:T(128)S(1)}) all-reduce(s32[64]{0:T(128)S(1)} %bitcast_dynamic-update-slice_fusion.1, s32[64]{0:T(128)S(1)} %dynamic-update-slice.1, s32[64]{0:T(128)S(1)} %dynamic-update-slice.2, ...), channel_id=2, replica_groups=mesh['dp'=4,'ctx'=64] {'ctx'}, use_global_device_ids=true, to_apply=%add.1 | all-reduce | flops 320 | bytes 2560 | tf_op jit(solution)/shard_map/all_gather | solution.py:15
  43.0 508.5 %while.60 = (s32[]{:T(128)}, s32[]{:T(128)}, s32[]{:T(128)}, s32[]{:T(128)}, s32[]{:T(128)}, /*index=5*/s32[64]{0:T(128)S(1)}, s32[64]{0:T(128)S(1)}, s32[64]{0:...) while((s32[]{:T(128)}, s32[]{:T(128)}, s32[]{:T(128)}, ...), condition=%wide.region_4.5_spmd, body=%wide.region_3.4_spmd.sunk | while | flops 18 | bytes 363 | solution.py:27
  556.6 81.9 %while.61 = (s32[]{:T(128)}, bf16[2,256,512]{2,1,0:T(8,128)(2,1)S(1)}, bf16[2,2304,512]{2,1,0:T(8,128)(2,1)}, s32[]{:T(128)}, s32[]{:T(128)}, /*index=5*/s32[]{:T(128)}, s32[]{:T(128)}, s32[]{:T(128)}) while((s32[]{:T(128)}, bf16[2,256,512]{2,1,0:T(8,128)(2,1)S(1)}, bf16[2,2304,512]{2,1,0:T(8,128)(2,1)}, s32[]{:T(128)}, s32[]{:T(128)}, ...), condition=%wide.region_1.2_spmd, body=%wide.region_0.0_spmd.sunk | while | flops 7 | bytes 4194491 | solution.py:143
  560.3 7.5 collective-permute-start
  570.2 9.0 collective-permute-start
  581.6 9.0 collective-permute-start
  593.0 9.0 collective-permute-start
  604.4 9.0 collective-permute-start
  615.7 9.0 collective-permute-start
  627.1 9.0 collective-permute-start
  638.5 6.8 copy.54
  656.1 144.7 %while.63 = (s32[]{:T(128)}, bf16[4,4,256,128]{3,2,1,0:T(8,128)(2,1)}, f32[4,2304,128]{1,2,0:T(8,128)}, f32[4,2304,128]{1,2,0:T(8,128)}, bf16[4,4,256,128]{2,3,1...) while((s32[]{:T(128)}, ...), condition=%wide.region_9.10_spmd.clone, body=%wide.region_5.9_spmd.clone.sunk | while | flops 3658453504 | bytes 69966016 | solution.py:87
  658.7 8.6 fusion.117
  685.5 6.8 fusion.120
  694.8 8.6 fusion.117
  721.7 6.8 fusion.120
  731.0 8.6 fusion.117
  757.8 6.8 fusion.120
  767.1 8.6 fusion.117
  794.0 6.8 fusion.120
  803.4 8.0 pad_maximum_fusion
  811.4 146.6 %while.62 = (s32[]{:T(128)}, f32[2,256,512]{2,1,0:T(8,128)}, f32[2,2304,512]{1,2,0:T(8,128)}, s32[]{:T(128)}, s32[]{:T(128)}, /*index=5*/s32[]{:T(128)}, s32[]{:T(128)}) while((s32[]{:T(128)}, f32[2,256,512]{2,1,0:T(8,128)}, f32[2,2304,512]{1,2,0:T(8,128)}, s32[]{:T(128)}, s32[]{:T(128)}, /*index=5*/s32[]{:T(128)}, s32[]{:T(128)}) %tuple.118), condition=%wide.region_11.12_spmd, body=%wide.region_10.11_spmd.sunk | while | flops 262150 | bytes 11534503 | solution.py:171
  830.5 12.0 collective-permute-done.1
  850.1 11.3 collective-permute-done.1
  868.9 11.3 collective-permute-done.1
  887.8 11.3 collective-permute-done.1
  906.6 11.3 collective-permute-done.1
  925.5 11.3 collective-permute-done.1
  944.4 11.3 collective-permute-done.1
  963.6 9.0 copy.71
  983.0 560.2 %reduce-scatter.4.cloned.1.call-done = f32[64,512]{1,0:T(8,128)} async-done(((f32[4096,512]{1,0:T(8,128)}), f32[64,512]{1,0:T(8,128)}) %reduce-scatter.4.cloned.1.call-update) | async-done | bytes 131088 | tf_op jit(solution)/shard_map/reduce_scatter | solution.py:181
  1543.2 14.9 all-gather.2
  (478 shorter events, 408.0 us)
Async XLA Ops:
  7.2 950.9 %copy-start = (bf16[1,256,4096]{2,1,0:T(8,128)(2,1)S(1)}, bf16[1,256,4096]{2,1,0:T(8,128)(2,1)}, u32[]{:S(2)}) copy-start(bf16[1,256,4096]{2,1,0:T(8,128)(2,1)} %param.16) | copy-start | bytes 6291460
  7.2 970.9 %all-gather.5.cloned.1.call-start = ((), (), s32[]{:S(2)}) async-start(), calls=%async_computation.1 | async-start | bytes 4259840 | tf_op jit(solution)/shard_map/all_gather | solution.py:177
  7.9 1535.3 %reduce-scatter.4.cloned.1.call-start = ((), (), s32[]{:S(2)}) async-start(), calls=%async_computation.2 | async-start | bytes 8519680 | tf_op jit(solution)/shard_map/reduce_scatter | solution.py:181
  556.6 2.8 collective-permute-start
  560.3 9.0 collective-permute-start
  570.2 10.5 collective-permute-start
  581.6 10.5 collective-permute-start
  593.0 10.5 collective-permute-start
  604.4 10.5 collective-permute-start
  615.7 10.5 collective-permute-start
  627.1 10.5 collective-permute-start
  645.3 5.0 copy-start.3
  658.7 8.6 copy-start.2
  672.7 2.1 copy-start.1
  694.8 8.6 copy-start.2
  708.8 2.1 copy-start.1
  730.9 8.6 copy-start.2
  745.0 2.1 copy-start.1
  767.1 8.6 copy-start.2
  781.1 2.1 copy-start.1
  811.4 11.5 collective-permute-start.1
  825.3 17.2 %collective-permute-start.1 = (f32[2,256,512]{2,1,0:T(8,128)}, f32[2,256,512]{2,1,0:T(8,128)}, u32[]{:S(2)}, u32[]{:S(2)}) collective-permute-start(f32[2,256,512]{2,1,0:T(8,128)} %get-tuple-element.817), channel_id=1, source_target_pairs={{1,0},{2,1},{3,2},{4,3},{5,4},{6,5},{7,6},{8,7},{9,8},{10,9},{11,1... | collective-permute-start | bytes 3145736 | tf_op jit(solution)/shard_map/while/body/eval_jaxpr/ppermute | solution.py:33
  844.9 16.4 %collective-permute-start.1 = (f32[2,256,512]{2,1,0:T(8,128)}, f32[2,256,512]{2,1,0:T(8,128)}, u32[]{:S(2)}, u32[]{:S(2)}) collective-permute-start(f32[2,256,512]{2,1,0:T(8,128)} %get-tuple-element.817), channel_id=1, source_target_pairs={{1,0},{2,1},{3,2},{4,3},{5,4},{6,5},{7,6},{8,7},{9,8},{10,9},{11,1... | collective-permute-start | bytes 3145736 | tf_op jit(solution)/shard_map/while/body/eval_jaxpr/ppermute | solution.py:33
  863.8 16.4 %collective-permute-start.1 = (f32[2,256,512]{2,1,0:T(8,128)}, f32[2,256,512]{2,1,0:T(8,128)}, u32[]{:S(2)}, u32[]{:S(2)}) collective-permute-start(f32[2,256,512]{2,1,0:T(8,128)} %get-tuple-element.817), channel_id=1, source_target_pairs={{1,0},{2,1},{3,2},{4,3},{5,4},{6,5},{7,6},{8,7},{9,8},{10,9},{11,1... | collective-permute-start | bytes 3145736 | tf_op jit(solution)/shard_map/while/body/eval_jaxpr/ppermute | solution.py:33
  882.7 16.4 %collective-permute-start.1 = (f32[2,256,512]{2,1,0:T(8,128)}, f32[2,256,512]{2,1,0:T(8,128)}, u32[]{:S(2)}, u32[]{:S(2)}) collective-permute-start(f32[2,256,512]{2,1,0:T(8,128)} %get-tuple-element.817), channel_id=1, source_target_pairs={{1,0},{2,1},{3,2},{4,3},{5,4},{6,5},{7,6},{8,7},{9,8},{10,9},{11,1... | collective-permute-start | bytes 3145736 | tf_op jit(solution)/shard_map/while/body/eval_jaxpr/ppermute | solution.py:33
  901.5 16.4 %collective-permute-start.1 = (f32[2,256,512]{2,1,0:T(8,128)}, f32[2,256,512]{2,1,0:T(8,128)}, u32[]{:S(2)}, u32[]{:S(2)}) collective-permute-start(f32[2,256,512]{2,1,0:T(8,128)} %get-tuple-element.817), channel_id=1, source_target_pairs={{1,0},{2,1},{3,2},{4,3},{5,4},{6,5},{7,6},{8,7},{9,8},{10,9},{11,1... | collective-permute-start | bytes 3145736 | tf_op jit(solution)/shard_map/while/body/eval_jaxpr/ppermute | solution.py:33
  920.4 16.4 %collective-permute-start.1 = (f32[2,256,512]{2,1,0:T(8,128)}, f32[2,256,512]{2,1,0:T(8,128)}, u32[]{:S(2)}, u32[]{:S(2)}) collective-permute-start(f32[2,256,512]{2,1,0:T(8,128)} %get-tuple-element.817), channel_id=1, source_target_pairs={{1,0},{2,1},{3,2},{4,3},{5,4},{6,5},{7,6},{8,7},{9,8},{10,9},{11,1... | collective-permute-start | bytes 3145736 | tf_op jit(solution)/shard_map/while/body/eval_jaxpr/ppermute | solution.py:33
  939.2 16.4 %collective-permute-start.1 = (f32[2,256,512]{2,1,0:T(8,128)}, f32[2,256,512]{2,1,0:T(8,128)}, u32[]{:S(2)}, u32[]{:S(2)}) collective-permute-start(f32[2,256,512]{2,1,0:T(8,128)} %get-tuple-element.817), channel_id=1, source_target_pairs={{1,0},{2,1},{3,2},{4,3},{5,4},{6,5},{7,6},{8,7},{9,8},{10,9},{11,1... | collective-permute-start | bytes 3145736 | tf_op jit(solution)/shard_map/while/body/eval_jaxpr/ppermute | solution.py:33
Sparse Core Ops, SparseCore 0:
  11.7 94.1 all-gather.4
  972.8 570.4 reduce-scatter.3
